TPU v7x, 32 devices: a whole 2x2x4 slice. The times are simulated.
32 devices in a mesh: img: 8 (over y, x, core), head: 4 (over z).
Axes of the slice: x: 2, y: 2, z: 4, core: 2. Of those that a mesh axis runs over, the one named last changes fastest.
Arguments:
- latents: bfloat16 [192, 64, 1024], P('img'), may hold values from -6 to 6
- media: bfloat16 [192, 256, 1024], P('img'), may hold values from -6 to 6
- valid_counts: int32 [192], P('img'), may hold values from 160 to 256, as said below
- w_query: bfloat16 [1024, 512], P(None, 'head'), may hold values from -0.1875 to 0.1875
- w_key: bfloat16 [1024, 512], P(None, 'head'), may hold values from -0.1875 to 0.1875
- w_value: bfloat16 [1024, 512], P(None, 'head'), may hold values from -0.1875 to 0.1875
- w_out: bfloat16 [1024, 512], P(None, 'head'), may hold values from -2 to 2
- w_up: bfloat16 [1024, 4096], P(None, 'head'), may hold values from -0.1875 to 0.1875
- w_down: bfloat16 [1024, 4096], P(None, 'head'), may hold values from -0.09375 to 0.09375
- norm_gains: float32 [3, 1024], replicated, may hold values from 0.5 to 1.5
- norm_biases: float32 [3, 1024], replicated, may hold values from -1.8 to 1.8
- cotangent: bfloat16 [192, 64, 1024], P('img'), may hold values from -6 to 6
Outputs:
- latents_out: bfloat16 [192, 64, 1024], P('img')
- latents_grad: bfloat16 [192, 64, 1024], P('img', 'head')
- media_grad: bfloat16 [192, 256, 1024], P('img', 'head')
- w_query_grad: float32 [1024, 512], P('img', 'head')
- w_key_grad: float32 [1024, 512], P('img', 'head')
- w_value_grad: float32 [1024, 512], P('img', 'head')
- w_out_grad: float32 [1024, 512], P('img', 'head')
- w_up_grad: float32 [1024, 4096], P('img', 'head')
- w_down_grad: float32 [1024, 4096], P('img', 'head')
- norm_gains_grad: float32 [3, 1024], P(None, ('img', 'head'))
- norm_biases_grad: float32 [3, 1024], P(None, ('img', 'head'))
Inputs may be any that keep to these rules, and one draw needn't show every extreme that they name: An image's valid patch keys are its first valid_counts patches; some image has exactly 256 and some exactly 160.
All inputs are finite; a program needn't handle non-finite values.
Results may differ from a plain program's by a relative error of at most 0.018.
Values may be sent and summed in bfloat16 or wider, within the bound.
No kernel may reach another device: no remote copies, remote signals or barrier semaphores. Data moves between devices by JAX's collectives and lax.ppermute only.
A program may use at most 192 MiB of HBM per device.

v0:
```python
import jax
import jax.numpy as jnp
from jax import lax
from jax.sharding import PartitionSpec as P

HEAD_DIM = 64
epsilon = 1e-05


def layer_norm(values, gain_row, bias_row):
    center = jnp.mean(values, axis=-1, keepdims=True)
    centered = values - center
    spread = jnp.mean(centered * centered, axis=-1, keepdims=True)
    return centered * lax.rsqrt(spread + epsilon) * gain_row + bias_row


def exact_gelu(values):
    return jax.nn.gelu(values, approximate=False)


def rows_share(values, member, count):
    return lax.dynamic_slice_in_dim(values, member * count, count, 1)


def body(
    latents,
    media,
    valid_counts,
    w_query,
    w_key,
    w_value,
    w_out,
    w_up,
    w_down,
    norm_gains,
    norm_biases,
    cotangent,
):
    groups = lax.axis_size("head")
    member = lax.axis_index("head")
    images, patches, model_width = media.shape
    latent_rows = latents.shape[1]
    share_rows = latent_rows // groups
    local_width = w_query.shape[1]
    local_heads = local_width // HEAD_DIM
    score_scale = HEAD_DIM ** (-0.5)
    latent_in = latents.astype(jnp.float32)
    media_in = media.astype(jnp.float32)
    media_normed = layer_norm(media_in, norm_gains[0], norm_biases[0]).astype(jnp.bfloat16)
    latent_normed = layer_norm(latent_in, norm_gains[1], norm_biases[1]).astype(jnp.bfloat16)
    joint_weight = jnp.concatenate([w_query, w_key, w_value], axis=1)
    media_kv = jnp.einsum(
        "ipd,de->ipe",
        media_normed,
        joint_weight[:, local_width:],
        preferred_element_type=jnp.float32,
    ).astype(jnp.bfloat16)
    latent_qkv = jnp.einsum(
        "ild,de->ile", latent_normed, joint_weight, preferred_element_type=jnp.float32
    ).astype(jnp.bfloat16)
    queries = latent_qkv[..., :local_width].reshape(images, latent_rows, local_heads, HEAD_DIM)
    key_rows = jnp.concatenate(
        [media_kv[..., :local_width], latent_qkv[..., local_width : 2 * local_width]], axis=1
    )
    key_rows = key_rows.reshape(images, patches + latent_rows, local_heads, HEAD_DIM)
    value_rows = jnp.concatenate(
        [media_kv[..., local_width:], latent_qkv[..., 2 * local_width :]], axis=1
    )
    value_rows = value_rows.reshape(images, patches + latent_rows, local_heads, HEAD_DIM)
    positions = lax.iota(jnp.int32, patches + latent_rows)
    allowed = (positions[None, :] < valid_counts[:, None]) | (positions[None, :] >= patches)
    scores = (
        jnp.einsum("ilhe,ikhe->ihlk", queries, key_rows, preferred_element_type=jnp.float32)
        * score_scale
    )
    scores = jnp.where(allowed[:, None, None, :], scores, -1e30)
    attention = jax.nn.softmax(scores, axis=-1)
    attention_low = attention.astype(jnp.bfloat16)
    attended = jnp.einsum(
        "ihlk,ikhe->ilhe", attention_low, value_rows, preferred_element_type=jnp.float32
    )
    attended = attended.astype(jnp.bfloat16).reshape(images, latent_rows, local_width)
    attn_part = jnp.einsum("ile,de->ild", attended, w_out, preferred_element_type=jnp.float32)
    residual = latent_in + lax.psum(attn_part.astype(jnp.bfloat16), "head").astype(jnp.float32)
    ffn_low = layer_norm(residual, norm_gains[2], norm_biases[2]).astype(jnp.bfloat16)
    pre_act = jnp.einsum("ild,df->ilf", ffn_low, w_up, preferred_element_type=jnp.float32)
    hidden, gelu_puller = jax.vjp(exact_gelu, pre_act)
    hidden_low = hidden.astype(jnp.bfloat16)
    mlp_part = jnp.einsum("ilf,df->ild", hidden_low, w_down, preferred_element_type=jnp.float32)
    latents_out = (
        residual + lax.psum(mlp_part.astype(jnp.bfloat16), "head").astype(jnp.float32)
    ).astype(jnp.bfloat16)
    upstream = cotangent.astype(jnp.float32)
    grad_down = jnp.einsum("ild,ilf->df", cotangent, hidden_low, preferred_element_type=jnp.float32)
    grad_hidden = jnp.einsum("ild,df->ilf", cotangent, w_down, preferred_element_type=jnp.float32)
    grad_pre = gelu_puller(grad_hidden)[0].astype(jnp.bfloat16)
    grad_up = jnp.einsum("ild,ilf->df", ffn_low, grad_pre, preferred_element_type=jnp.float32)
    grad_ffn_part = jnp.einsum("ilf,df->ild", grad_pre, w_up, preferred_element_type=jnp.float32)
    grad_ffn = lax.psum(grad_ffn_part.astype(jnp.bfloat16), "head").astype(jnp.float32)
    norm_puller = jax.vjp(layer_norm, residual, norm_gains[2], norm_biases[2])[1]
    grad_from_norm, gain_ffn, bias_ffn = norm_puller(grad_ffn)
    grad_residual = upstream + grad_from_norm
    grad_low = grad_residual.astype(jnp.bfloat16)
    grad_residual_share = rows_share(grad_residual, member, share_rows)
    gain_ffn = gain_ffn / groups
    bias_ffn = bias_ffn / groups
    grad_wout = jnp.einsum("ild,ile->de", grad_low, attended, preferred_element_type=jnp.float32)
    grad_attended = jnp.einsum("ild,de->ile", grad_low, w_out, preferred_element_type=jnp.float32)
    grad_attended = grad_attended.astype(jnp.bfloat16).reshape(
        images, latent_rows, local_heads, HEAD_DIM
    )
    grad_values = jnp.einsum(
        "ihlk,ilhe->ikhe", attention_low, grad_attended, preferred_element_type=jnp.float32
    )
    grad_attention = jnp.einsum(
        "ilhe,ikhe->ihlk", grad_attended, value_rows, preferred_element_type=jnp.float32
    )
    row_total = jnp.sum(attention * grad_attention, axis=-1, keepdims=True)
    grad_scores = (attention * (grad_attention - row_total)).astype(jnp.bfloat16)
    grad_queries = (
        jnp.einsum("ihlk,ikhe->ilhe", grad_scores, key_rows, preferred_element_type=jnp.float32)
        * score_scale
    )
    grad_keys = (
        jnp.einsum("ihlk,ilhe->ikhe", grad_scores, queries, preferred_element_type=jnp.float32)
        * score_scale
    )
    grad_queries = grad_queries.astype(jnp.bfloat16).reshape(images, latent_rows, local_width)
    grad_keys = grad_keys.astype(jnp.bfloat16).reshape(images, patches + latent_rows, local_width)
    grad_values = grad_values.astype(jnp.bfloat16).reshape(
        images, patches + latent_rows, local_width
    )
    media_grad_kv = jnp.concatenate([grad_keys[:, :patches], grad_values[:, :patches]], axis=2)
    latent_grad_qkv = jnp.concatenate(
        [grad_queries, grad_keys[:, patches:], grad_values[:, patches:]], axis=2
    )
    media_weight_grad = jnp.einsum(
        "ipd,ipe->de", media_normed, media_grad_kv, preferred_element_type=jnp.float32
    )
    latent_weight_grad = jnp.einsum(
        "ild,ile->de", latent_normed, latent_grad_qkv, preferred_element_type=jnp.float32
    )
    grad_wq = latent_weight_grad[:, :local_width]
    grad_wk = (
        media_weight_grad[:, :local_width] + latent_weight_grad[:, local_width : 2 * local_width]
    )
    grad_wv = media_weight_grad[:, local_width:] + latent_weight_grad[:, 2 * local_width :]
    grads_out = (
        lax.psum_scatter(grad_wq, "img", scatter_dimension=0, tiled=True),
        lax.psum_scatter(grad_wk, "img", scatter_dimension=0, tiled=True),
        lax.psum_scatter(grad_wv, "img", scatter_dimension=0, tiled=True),
        lax.psum_scatter(grad_wout, "img", scatter_dimension=0, tiled=True),
        lax.psum_scatter(grad_up, "img", scatter_dimension=0, tiled=True),
        lax.psum_scatter(grad_down, "img", scatter_dimension=0, tiled=True),
    )
    media_part = jnp.einsum(
        "ipe,de->ipd",
        media_grad_kv,
        joint_weight[:, local_width:],
        preferred_element_type=jnp.float32,
    )
    latent_part = jnp.einsum(
        "ile,de->ild", latent_grad_qkv, joint_weight, preferred_element_type=jnp.float32
    )
    media_share, latent_share = (
        lax.psum_scatter(
            media_part.astype(jnp.bfloat16), "head", scatter_dimension=1, tiled=True
        ).astype(jnp.float32),
        lax.psum_scatter(
            latent_part.astype(jnp.bfloat16), "head", scatter_dimension=1, tiled=True
        ).astype(jnp.float32),
    )
    media_rows = patches // groups
    media_puller = jax.vjp(
        layer_norm, rows_share(media_in, member, media_rows), norm_gains[0], norm_biases[0]
    )[1]
    grad_media_in, gain_media, bias_media = media_puller(media_share)
    latent_puller = jax.vjp(
        layer_norm, rows_share(latent_in, member, share_rows), norm_gains[1], norm_biases[1]
    )[1]
    grad_latent_norm, gain_latent, bias_latent = latent_puller(latent_share)
    latents_grad = (grad_residual_share + grad_latent_norm).astype(jnp.bfloat16)
    media_grad = grad_media_in.astype(jnp.bfloat16)
    gain_terms = jnp.stack([gain_media, gain_latent, gain_ffn])
    bias_terms = jnp.stack([bias_media, bias_latent, bias_ffn])
    gain_total, bias_total = (
        lax.psum_scatter(gain_terms, ("img", "head"), scatter_dimension=1, tiled=True),
        lax.psum_scatter(bias_terms, ("img", "head"), scatter_dimension=1, tiled=True),
    )
    return (
        latents_out,
        latents_grad,
        media_grad,
        grads_out[0],
        grads_out[1],
        grads_out[2],
        grads_out[3],
        grads_out[4],
        grads_out[5],
        gain_total,
        bias_total,
    )


def solution(mesh):
    return jax.shard_map(
        body,
        mesh=mesh,
        in_specs=(
            P("img", None, None),
            P("img", None, None),
            P("img"),
            P(None, "head"),
            P(None, "head"),
            P(None, "head"),
            P(None, "head"),
            P(None, "head"),
            P(None, "head"),
            P(),
            P(),
            P("img", None, None),
        ),
        out_specs=(
            P("img", None, None),
            P("img", "head", None),
            P("img", "head", None),
            P("img", "head"),
            P("img", "head"),
            P("img", "head"),
            P("img", "head"),
            P("img", "head"),
            P("img", "head"),
            P(None, ("img", "head")),
            P(None, ("img", "head")),
        ),
        check_vma=False,
    )
```

profile of v0, /device:TPU:0, one launch (start us, length us, event | category | flops | bytes accessed | tf_op | source)
XLA Modules:
  0.0 1304.9 jit_solution(8463983802196653508)
XLA Ops:
  13.8 6.3 convert_reduce_fusion
  20.2 8.3 multiply_reduce_fusion
  32.9 8.5 fusion.23
  53.2 5.5 fusion.74
  65.9 123.6 %all-reduce.4.cloned.1.call-done = bf16[24,64,1024]{2,1,0:T(8,128)(2,1)} async-done(((bf16[24,64,1024]{2,1,0:T(8,128)(2,1)}), bf16[24,64,1024]{2,1,0:T(8,128)(2,1)}) %all-reduce.4.cloned.1.call-update) | async-done | bytes 3145744 | tf_op jit(solution)/shard_map/psum | solution.py:84
  195.6 5.7 convert_reduce_fusion.4
  201.3 14.4 %multiply_convert_fusion = (bf16[24,64,1024]{2,1,0:T(8,128)(2,1)S(1)}, f32[24,64,1024]{2,1,0:T(8,128)S(1)}) fusion(f32[24,64,1024]{2,1,0:T(8,128)S(1)} %get-tuple-element.86, u32[64,1024]{1,0:T(8,128)S(1)} %get-tuple-element.55, u32[64,1024]{1,0:T(8,128)S(1)} %get-tuple-element.54), kind=kLoop, calls=%fused_computation.35 | loop fusion | flops 106954752 | bytes 16252928 | tf_op jit(solution)/shard_map/convert_element_type | solution.py:88
  215.7 6.4 add_convert_fusion.4
  222.0 6.7 convolution_convert_fusion.1
  233.7 222.0 %all-reduce.6.cloned.1.call-done = (bf16[24,64,1024]{2,1,0:T(8,128)(2,1)}, bf16[24,64,1024]{2,1,0:T(8,128)(2,1)}) async-done(((bf16[24,64,1024]{2,1,0:T(8,128)(2,1)}, bf16[24,64,1024]{2,1,0:T(8,128)(2,1)}), (bf16[24,64,1024]{2,1,0:T(8,128)(2,1)}, bf16[24,64,1024]{2,1,0:T(8,128)(2,1)})) %all-reduce.6.cloned.1.call-update) | async-done | bytes 6291472 | tf_op jit(solution)/shard_map/psum | solution.py:91
  455.7 5.4 convert_reduce_fusion.2
  461.1 6.5 fusion.10
  502.0 8.5 convolution_convert_fusion
  510.6 8.4 convolution_bitcast_fusion
  519.0 5.2 convert_element_type.105
  524.3 14.3 %convert_element_type.106 = f32[24,256,1024]{2,1,0:T(8,128)} convert(bf16[24,256,1024]{2,1,0:T(8,128)(2,1)} %param.13) | non-fusion elementwise | flops 6291456 | bytes 37748736 | tf_op jit(solution)/shard_map/convert_element_type | solution.py:48
  543.4 10.0 reduce-scatter.15.cloned.1.call-done
  558.1 209.2 %reduce-scatter.17.cloned.1.call-done = bf16[24,64,1024]{2,1,0:T(8,128)(2,1)} async-done(((bf16[24,256,1024]{2,1,0:T(8,128)(2,1)}), bf16[24,64,1024]{2,1,0:T(8,128)(2,1)}) %reduce-scatter.17.cloned.1.call-update) | async-done | bytes 3145744 | tf_op jit(solution)/shard_map/reduce_scatter | solution.py:166
  767.3 6.1 multiply_reduce_fusion.1
  773.5 5.8 fusion.11
  781.9 10.5 convolution_bitcast_fusion.1
  792.5 6.3 fusion.47
  798.8 9.2 fusion.43
  814.8 7.8 reduce-scatter.29.cloned.1.call-done
  828.1 6.1 add_convert_fusion.3
  834.2 126.4 %reduce-scatter.31.cloned.1.call-done = f32[32,3]{1,0:T(8,128)} async-done(((f32[1024,3]{1,0:T(8,128)}), f32[32,3]{1,0:T(8,128)}) %reduce-scatter.31.cloned.1.call-update) | async-done | bytes 400
  961.9 133.5 %reduce-scatter.33.cloned.1.call-done = f32[32,3]{1,0:T(8,128)} async-done(((f32[1024,3]{1,0:T(8,128)}), f32[32,3]{1,0:T(8,128)}) %reduce-scatter.33.cloned.1.call-update) | async-done | bytes 400
  1096.9 49.8 %reduce-scatter.27.cloned.1.call-done = f32[128,1024]{1,0:T(8,128)} async-done(((f32[1024,1024]{1,0:T(8,128)}), f32[128,1024]{1,0:T(8,128)}) %reduce-scatter.27.cloned.1.call-update) | async-done | bytes 524304 | tf_op jit(solution)/shard_map/reduce_scatter | solution.py:153
  1146.6 37.8 %reduce-scatter.25.cloned.1.call-done = f32[128,128]{1,0:T(8,128)} async-done(((f32[1024,128]{1,0:T(8,128)}), f32[128,128]{1,0:T(8,128)}) %reduce-scatter.25.cloned.1.call-update) | async-done | bytes 65552 | tf_op jit(solution)/shard_map/reduce_scatter | solution.py:152
  1184.5 37.7 %reduce-scatter.23.cloned.1.call-done = f32[128,128]{1,0:T(8,128)} async-done(((f32[1024,128]{1,0:T(8,128)}), f32[128,128]{1,0:T(8,128)}) %reduce-scatter.23.cloned.1.call-update) | async-done | bytes 65552 | tf_op jit(solution)/shard_map/reduce_scatter | solution.py:151
  1222.1 37.8 %reduce-scatter.21.cloned.1.call-done = f32[128,128]{1,0:T(8,128)} async-done(((f32[1024,128]{1,0:T(8,128)}), f32[128,128]{1,0:T(8,128)}) %reduce-scatter.21.cloned.1.call-update) | async-done | bytes 65552 | tf_op jit(solution)/shard_map/reduce_scatter | solution.py:150
  1259.9 37.7 %reduce-scatter.19.cloned.1.call-done = f32[128,128]{1,0:T(8,128)} async-done(((f32[1024,128]{1,0:T(8,128)}), f32[128,128]{1,0:T(8,128)}) %reduce-scatter.19.cloned.1.call-update) | async-done | bytes 65552 | tf_op jit(solution)/shard_map/reduce_scatter | solution.py:149
  (211 shorter events, 101.9 us)
Async XLA Ops:
  7.2 188.4 %copy-start = (bf16[1024,1024]{1,0:T(8,128)(2,1)S(1)}, bf16[1024,1024]{1,0:T(8,128)(2,1)}, u32[]{:S(2)}) copy-start(bf16[1024,1024]{1,0:T(8,128)(2,1)} %param.19) | copy-start | bytes 6291460
  7.2 182.3 %all-reduce.4.cloned.1.call-start = ((), (), s32[]{:S(2)}) async-start(), calls=%async_computation.10 | async-start | bytes 6291456 | tf_op jit(solution)/shard_map/psum | solution.py:84
  10.2 18.9 %copy-start.43 = (f32[24,64]{1,0:T(8,128)}, f32[24,64]{1,0:T(8,128)S(1)}, u32[]{:S(2)}) copy-start(f32[24,64]{1,0:T(8,128)S(1)} %broadcast_multiply_fusion.4) | copy-start | bytes 18436
  13.1 16.0 %copy-start.47 = (f32[24,64]{1,0:T(8,128)}, f32[24,64]{1,0:T(8,128)S(1)}, u32[]{:S(2)}) copy-start(f32[24,64]{1,0:T(8,128)S(1)} %add_rsqrt_fusion.1) | copy-start | bytes 18436
  13.2 15.9 %copy-start.41 = (f32[1,1024]{1,0:T(1,128)}, f32[1,1024]{1,0:T(1,128)S(1)}, u32[]{:S(2)}) copy-start(f32[1,1024]{1,0:T(1,128)S(1)} %get-tuple-element.76) | copy-start | bytes 12292
  13.2 454.5 %copy-start.39 = (f32[1,1024]{1,0:T(1,128)}, f32[1,1024]{1,0:T(1,128)S(1)}, u32[]{:S(2)}) copy-start(f32[1,1024]{1,0:T(1,128)S(1)} %get-tuple-element.74) | copy-start | bytes 12292
  13.8 15.3 %copy-start.50 = (f32[1,1024]{1,0:T(1,128)}, f32[1,1024]{1,0:T(1,128)S(1)}, u32[]{:S(2)}) copy-start(f32[1,1024]{1,0:T(1,128)S(1)} %get-tuple-element.79) | copy-start | bytes 12292
  32.9 20.3 %copy-start.17 = (bf16[24,64,128]{1,2,0:T(8,128)(2,1)}, bf16[24,64,128]{1,2,0:T(8,128)(2,1)S(1)}, u32[]{:S(2)}) copy-start(bf16[24,64,128]{1,2,0:T(8,128)(2,1)S(1)} %copy.81) | copy-start | bytes 1179652
  65.6 130.0 %copy-start.53 = (f32[1,1024]{1,0:T(1,128)S(1)}, f32[1,1024]{1,0:T(1,128)}, u32[]{:S(2)}) copy-start(f32[1,1024]{1,0:T(1,128)} %get-tuple-element.77) | copy-start | bytes 12292
  65.6 390.1 %all-reduce.6.cloned.1.call-start = ((), (), s32[]{:S(2)}) async-start(), calls=%async_computation.21 | async-start | bytes 12582912 | tf_op jit(solution)/shard_map/psum | solution.py:91
  201.2 14.4 %copy-start.14 = (bf16[24,64,1024]{2,1,0:T(8,128)(2,1)S(1)}, bf16[24,64,1024]{2,1,0:T(8,128)(2,1)}, u32[]{:S(2)}) copy-start(bf16[24,64,1024]{2,1,0:T(8,128)(2,1)} %param.23) | copy-start | bytes 9437188
  201.3 14.4 %copy-start.56 = (bf16[1024,1024]{1,0:T(8,128)(2,1)S(1)}, bf16[1024,1024]{1,0:T(8,128)(2,1)}, u32[]{:S(2)}) copy-start(bf16[1024,1024]{1,0:T(8,128)(2,1)} %param.20) | copy-start | bytes 6291460
  215.6 13.1 %copy-start.19 = (bf16[24,64,1024]{2,1,0:T(8,128)(2,1)}, bf16[24,64,1024]{2,1,0:T(8,128)(2,1)S(1)}, u32[]{:S(2)}) copy-start(bf16[24,64,1024]{2,1,0:T(8,128)(2,1)S(1)} %get-tuple-element.62) | copy-start | bytes 9437188
  233.6 319.7 %reduce-scatter.15.cloned.1.call-start = ((), (), s32[]{:S(2)}) async-start(), calls=%async_computation.11 | async-start | bytes 3932160 | tf_op jit(solution)/shard_map/reduce_scatter | solution.py:169
  455.7 12.0 copy-start.16
  493.9 273.5 %reduce-scatter.17.cloned.1.call-start = ((), (), s32[]{:S(2)}) async-start(), calls=%async_computation.12 | async-start | bytes 15728640 | tf_op jit(solution)/shard_map/reduce_scatter | solution.py:166
  510.5 312.2 %reduce-scatter.29.cloned.1.call-start = ((), (), s32[]{:S(2)}) async-start(), calls=%async_computation.18 | async-start | bytes 4718592 | tf_op jit(solution)/shard_map/reduce_scatter | solution.py:154
  519.0 441.6 %reduce-scatter.31.cloned.1.call-start = ((), (), s32[]{:S(2)}) async-start(), calls=%async_computation.19 | async-start | bytes 540672
  538.6 14.7 %copy-start.42 = (f32[1,1024]{1,0:T(1,128)S(1)}, f32[1,1024]{1,0:T(1,128)}, u32[]{:S(2)}) copy-start(f32[1,1024]{1,0:T(1,128)} %copy-done.41) | copy-start | bytes 12292
  773.4 18.9 %copy-start.33 = (f32[24,64]{1,0:T(8,128)}, f32[24,64]{1,0:T(8,128)S(1)}, u32[]{:S(2)}) copy-start(f32[24,64]{1,0:T(8,128)S(1)} %get-tuple-element.80) | copy-start | bytes 18436
  773.4 18.9 %copy-start.35 = (f32[24,64]{1,0:T(8,128)}, f32[24,64]{1,0:T(8,128)S(1)}, u32[]{:S(2)}) copy-start(f32[24,64]{1,0:T(8,128)S(1)} %get-tuple-element.81) | copy-start | bytes 18436
  780.4 315.1 %reduce-scatter.33.cloned.1.call-start = ((), (), s32[]{:S(2)}) async-start(), calls=%async_computation.20 | async-start | bytes 540672
  781.6 365.1 %reduce-scatter.27.cloned.1.call-start = ((), (), s32[]{:S(2)}) async-start(), calls=%async_computation.17 | async-start | bytes 4718592 | tf_op jit(solution)/shard_map/reduce_scatter | solution.py:153
  792.4 392.0 %reduce-scatter.25.cloned.1.call-start = ((), (), s32[]{:S(2)}) async-start(), calls=%async_computation.16 | async-start | bytes 589824 | tf_op jit(solution)/shard_map/reduce_scatter | solution.py:152
  808.1 414.1 %reduce-scatter.23.cloned.1.call-start = ((), (), s32[]{:S(2)}) async-start(), calls=%async_computation.15 | async-start | bytes 589824 | tf_op jit(solution)/shard_map/reduce_scatter | solution.py:151
  812.2 12.5 copy-start.11
  812.2 15.8 %copy-start.45 = (f32[24,64]{1,0:T(8,128)S(1)}, f32[24,64]{1,0:T(8,128)}, u32[]{:S(2)}) copy-start(f32[24,64]{1,0:T(8,128)} %get-tuple-element.45) | copy-start | bytes 18436
  812.2 15.8 %copy-start.34 = (f32[24,64]{1,0:T(8,128)S(1)}, f32[24,64]{1,0:T(8,128)}, u32[]{:S(2)}) copy-start(f32[24,64]{1,0:T(8,128)} %copy-done.33) | copy-start | bytes 18436
  812.2 15.8 %copy-start.36 = (f32[24,64]{1,0:T(8,128)S(1)}, f32[24,64]{1,0:T(8,128)}, u32[]{:S(2)}) copy-start(f32[24,64]{1,0:T(8,128)} %copy-done.35) | copy-start | bytes 18436
  813.5 446.4 %reduce-scatter.21.cloned.1.call-start = ((), (), s32[]{:S(2)}) async-start(), calls=%async_computation.14 | async-start | bytes 589824 | tf_op jit(solution)/shard_map/reduce_scatter | solution.py:150
  814.2 483.4 %reduce-scatter.19.cloned.1.call-start = ((), (), s32[]{:S(2)}) async-start(), calls=%async_computation.13 | async-start | bytes 589824 | tf_op jit(solution)/shard_map/reduce_scatter | solution.py:149
  828.0 469.6 %copy-start.1 = (bf16[1024,1024]{1,0:T(8,128)(2,1)S(1)}, bf16[1024,1024]{1,0:T(8,128)(2,1)}, u32[]{:S(2)}) copy-start(bf16[1024,1024]{1,0:T(8,128)(2,1)} %param.19) | copy-start | bytes 6291460
  (40 other events, 249.5 us)
Sparse Core Ops, SparseCore 0:
  65.7 123.7 all-reduce.3
  233.7 221.8 all-reduce.5
  494.0 59.2 reduce-scatter.14
  555.5 211.7 reduce-scatter.16
  770.5 52.0 reduce-scatter.28
  824.8 135.7 reduce-scatter.30
  962.8 132.6 reduce-scatter.32
  1099.4 47.1 reduce-scatter.26
  1150.3 34.1 reduce-scatter.24
  1188.0 34.1 reduce-scatter.22
  1225.8 34.1 reduce-scatter.20
  1263.5 34.1 reduce-scatter.18
where the time goes:
time: 1310 us; the launch traced here: 1300 us
  waiting for transfers between devices  1030 us (79%)
  other arithmetic  112 us (9%)
  matrix products  107 us (8%)
  local copies, waits for them, and re-layouts  34.5 us (3%)
  between operations  15.6 us (1%)
    unnamed x14, waiting for transfers between devices  261 us
    psum x1, waiting for transfers between devices, body(): lax.psum(mlp_part.astype(jnp.bfloat16), 'head').astype(jnp.float32)  222 us
    reduce_scatter x1, waiting for transfers between devices, body(): lax.psum_scatter(media_part.astype(jnp.bfloat16), 'head', scatter_dimensi...  209 us
    psum x1, waiting for transfers between devices, body(): lax.psum(attn_part.astype(jnp.bfloat16), 'head').astype(jnp.float32)  124 us
    reduce_scatter x1, waiting for transfers between devices, body(): lax.psum_scatter(grad_up, 'img', scatter_dimension=0, tiled=True)  49.8 us
    reduce_scatter x1, waiting for transfers between devices, body(): lax.psum_scatter(grad_wout, 'img', scatter_dimension=0, tiled=True)  37.8 us
    reduce_scatter x1, waiting for transfers between devices, body(): lax.psum_scatter(grad_wk, 'img', scatter_dimension=0, tiled=True)  37.8 us
    reduce_scatter x1, waiting for transfers between devices, body(): lax.psum_scatter(grad_wq, 'img', scatter_dimension=0, tiled=True)  37.7 us
  transfers between devices with their start and end apart: 12, of which 12 were waited for; matrix products, arithmetic and copies ran while one was open for 9% of the time, Pallas kernels for 0%

commit v1 on v0

--- a/solution.py
+++ b/solution.py
@@ -1,10 +1,19 @@
+import functools
 import jax
 import jax.numpy as jnp
 from jax import lax
 from jax.sharding import PartitionSpec as P
+from jax.lax import all_gather
 
 HEAD_DIM = 64
 epsilon = 1e-05
+
+
+def divide_cards_over_axis(x_local, group_axis):
+    return jnp.sum(all_gather(x_local, group_axis), axis=0)
+
+
+get_shards = functools.partial(divide_cards_over_axis, group_axis="head")
 
 
 def layer_norm(values, gain_row, bias_row):
@@ -87,9 +96,9 @@
     hidden, gelu_puller = jax.vjp(exact_gelu, pre_act)
     hidden_low = hidden.astype(jnp.bfloat16)
     mlp_part = jnp.einsum("ilf,df->ild", hidden_low, w_down, preferred_element_type=jnp.float32)
-    latents_out = (
-        residual + lax.psum(mlp_part.astype(jnp.bfloat16), "head").astype(jnp.float32)
-    ).astype(jnp.bfloat16)
+    latents_out = (residual + get_shards(mlp_part.astype(jnp.bfloat16)).astype(jnp.float32)).astype(
+        jnp.bfloat16
+    )
     upstream = cotangent.astype(jnp.float32)
     grad_down = jnp.einsum("ild,ilf->df", cotangent, hidden_low, preferred_element_type=jnp.float32)
     grad_hidden = jnp.einsum("ild,df->ilf", cotangent, w_down, preferred_element_type=jnp.float32)

time: 1310 us -> 1420 us (1.084)
  waiting for transfers between devices: 1030 us -> 1130 us
  other arithmetic: 112 us -> 127 us
    all_gather x0 -> x1, waiting for transfers between devices: none -> 207 us  [divide_cards_over_axis(): return jnp.sum(all_gather(x_local, group_axis), axis=0)]
    psum x1, waiting for transfers between devices: 222 us -> 112 us  [body(): lax.psum(grad_ffn_part.astype(jnp.bfloat16), 'head').astype(jnp.float32)]
    unnamed x14 -> x15, waiting for transfers between devices: 261 us -> 260 us
  transfers between devices with their start and end apart: 12 -> 13, of which waited for: 12 -> 13; matrix products, arithmetic and copies ran while one was open for 9% -> 9% of each run, Pallas kernels for 0% -> 0%
where the time goes in v1:
time: 1420 us
  waiting for transfers between devices  1130 us (80%)
  other arithmetic  127 us (9%)
  matrix products  108 us (8%)
  local copies, waits for them, and re-layouts  35.9 us (3%)
  between operations  15 us (1%)
    unnamed x15, waiting for transfers between devices  260 us
    reduce_scatter x1, waiting for transfers between devices, body(): lax.psum_scatter(media_part.astype(jnp.bfloat16), 'head', scatter_dimensi...  209 us
    all_gather x1, waiting for transfers between devices, divide_cards_over_axis(): return jnp.sum(all_gather(x_local, group_axis), axis=0)  207 us
    psum x1, waiting for transfers between devices, body(): lax.psum(attn_part.astype(jnp.bfloat16), 'head').astype(jnp.float32)  123 us
    psum x1, waiting for transfers between devices, body(): lax.psum(grad_ffn_part.astype(jnp.bfloat16), 'head').astype(jnp.float32)  112 us
    reduce_scatter x1, waiting for transfers between devices, body(): lax.psum_scatter(grad_up, 'img', scatter_dimension=0, tiled=True)  50.1 us
    reduce_scatter x1, waiting for transfers between devices, body(): lax.psum_scatter(grad_wv, 'img', scatter_dimension=0, tiled=True)  37.8 us
    reduce_scatter x1, waiting for transfers between devices, body(): lax.psum_scatter(grad_wq, 'img', scatter_dimension=0, tiled=True)  37.8 us
  transfers between devices with their start and end apart: 13, of which 13 were waited for; matrix products, arithmetic and copies ran while one was open for 9% of the time, Pallas kernels for 0%

profile of v1, /device:TPU:0, one launch (start us, length us, event | category | flops | bytes accessed | tf_op | source)
XLA Modules:
  0.0 1418.1 jit_solution(12312669485396473193)
XLA Ops:
  13.8 6.3 convert_reduce_fusion
  20.2 8.4 multiply_reduce_fusion
  33.1 8.5 fusion.23
  53.3 5.5 fusion.74
  66.2 123.3 %all-reduce.3.cloned.1.call-done = bf16[24,64,1024]{2,1,0:T(8,128)(2,1)} async-done(((bf16[24,64,1024]{2,1,0:T(8,128)(2,1)}), bf16[24,64,1024]{2,1,0:T(8,128)(2,1)}) %all-reduce.3.cloned.1.call-update) | async-done | bytes 3145744 | tf_op jit(solution)/shard_map/psum | solution.py:93
  195.6 5.7 convert_reduce_fusion.4
  201.3 14.8 %multiply_convert_fusion = (bf16[24,64,1024]{2,1,0:T(8,128)(2,1)}, f32[24,64,1024]{2,1,0:T(8,128)S(1)}) fusion(f32[24,64,1024]{2,1,0:T(8,128)S(1)} %get-tuple-element.84, u32[64,1024]{1,0:T(8,128)S(1)} %get-tuple-element.55, u32[64,1024]{1,0:T(8,128)S(1)} %get-tuple-element.54), kind=kLoop, calls=%fused_computation.35 | loop fusion | flops 106954752 | bytes 16252928 | tf_op jit(solution)/shard_map/convert_element_type | solution.py:97
  227.9 7.7 convolution_convert_fusion.2
  235.7 112.4 %all-reduce.5.cloned.1.call-done = bf16[24,64,1024]{2,1,0:T(8,128)(2,1)} async-done(((bf16[24,64,1024]{2,1,0:T(8,128)(2,1)}), bf16[24,64,1024]{2,1,0:T(8,128)(2,1)}) %all-reduce.5.cloned.1.call-update) | async-done | bytes 3145744 | tf_op jit(solution)/shard_map/psum | solution.py:108
  353.5 6.2 fusion.10
  359.8 207.1 %all-gather.3.cloned.1.call-done = bf16[96,64,1024]{2,1,0:T(8,128)(2,1)} async-done(((bf16[24,64,1024]{2,1,0:T(8,128)(2,1)}), bf16[96,64,1024]{2,1,0:T(8,128)(2,1)}) %all-gather.3.cloned.1.call-update) | async-done | bytes 12582928 | tf_op jit(solution)/shard_map/all_gather | solution.py:13
  566.9 10.6 reduce_sum.237
  577.4 8.5 add_add_fusion.2
  616.2 8.5 convolution_convert_fusion
  624.9 8.4 convolution_bitcast_fusion
  638.6 14.4 %convert_element_type.108 = f32[24,256,1024]{2,1,0:T(8,128)} convert(bf16[24,256,1024]{2,1,0:T(8,128)(2,1)} %param.13) | non-fusion elementwise | flops 6291456 | bytes 37748736 | tf_op jit(solution)/shard_map/convert_element_type | solution.py:57
  657.8 9.3 reduce-scatter.15.cloned.1.call-done
  671.9 209.2 %reduce-scatter.17.cloned.1.call-done = bf16[24,64,1024]{2,1,0:T(8,128)(2,1)} async-done(((bf16[24,256,1024]{2,1,0:T(8,128)(2,1)}), bf16[24,64,1024]{2,1,0:T(8,128)(2,1)}) %reduce-scatter.17.cloned.1.call-update) | async-done | bytes 3145744 | tf_op jit(solution)/shard_map/reduce_scatter | solution.py:175
  881.1 6.1 multiply_reduce_fusion.1
  887.2 5.8 fusion.11
  895.4 10.5 convolution_bitcast_fusion.1
  906.0 6.3 fusion.47
  912.4 9.4 fusion.43
  927.8 8.6 reduce-scatter.29.cloned.1.call-done
  941.9 6.1 add_convert_fusion.3
  948.0 126.6 %reduce-scatter.31.cloned.1.call-done = f32[32,3]{1,0:T(8,128)} async-done(((f32[1024,3]{1,0:T(8,128)}), f32[32,3]{1,0:T(8,128)}) %reduce-scatter.31.cloned.1.call-update) | async-done | bytes 400
  1075.9 133.0 %reduce-scatter.33.cloned.1.call-done = f32[32,3]{1,0:T(8,128)} async-done(((f32[1024,3]{1,0:T(8,128)}), f32[32,3]{1,0:T(8,128)}) %reduce-scatter.33.cloned.1.call-update) | async-done | bytes 400
  1210.3 50.1 %reduce-scatter.27.cloned.1.call-done = f32[128,1024]{1,0:T(8,128)} async-done(((f32[1024,1024]{1,0:T(8,128)}), f32[128,1024]{1,0:T(8,128)}) %reduce-scatter.27.cloned.1.call-update) | async-done | bytes 524304 | tf_op jit(solution)/shard_map/reduce_scatter | solution.py:162
  1260.4 37.6 %reduce-scatter.25.cloned.1.call-done = f32[128,128]{1,0:T(8,128)} async-done(((f32[1024,128]{1,0:T(8,128)}), f32[128,128]{1,0:T(8,128)}) %reduce-scatter.25.cloned.1.call-update) | async-done | bytes 65552 | tf_op jit(solution)/shard_map/reduce_scatter | solution.py:161
  1298.0 37.8 %reduce-scatter.23.cloned.1.call-done = f32[128,128]{1,0:T(8,128)} async-done(((f32[1024,128]{1,0:T(8,128)}), f32[128,128]{1,0:T(8,128)}) %reduce-scatter.23.cloned.1.call-update) | async-done | bytes 65552 | tf_op jit(solution)/shard_map/reduce_scatter | solution.py:160
  1335.9 37.7 %reduce-scatter.21.cloned.1.call-done = f32[128,128]{1,0:T(8,128)} async-done(((f32[1024,128]{1,0:T(8,128)}), f32[128,128]{1,0:T(8,128)}) %reduce-scatter.21.cloned.1.call-update) | async-done | bytes 65552 | tf_op jit(solution)/shard_map/reduce_scatter | solution.py:159
  1373.5 37.8 %reduce-scatter.19.cloned.1.call-done = f32[128,128]{1,0:T(8,128)} async-done(((f32[1024,128]{1,0:T(8,128)}), f32[128,128]{1,0:T(8,128)}) %reduce-scatter.19.cloned.1.call-update) | async-done | bytes 65552 | tf_op jit(solution)/shard_map/reduce_scatter | solution.py:158
  (207 shorter events, 114.8 us)
Async XLA Ops:
  7.2 188.4 %copy-start = (bf16[1024,1024]{1,0:T(8,128)(2,1)S(1)}, bf16[1024,1024]{1,0:T(8,128)(2,1)}, u32[]{:S(2)}) copy-start(bf16[1024,1024]{1,0:T(8,128)(2,1)} %param.19) | copy-start | bytes 6291460
  7.2 182.3 %all-reduce.3.cloned.1.call-start = ((), (), s32[]{:S(2)}) async-start(), calls=%async_computation.10 | async-start | bytes 6291456 | tf_op jit(solution)/shard_map/psum | solution.py:93
  10.2 19.0 %copy-start.38 = (f32[24,64]{1,0:T(8,128)}, f32[24,64]{1,0:T(8,128)S(1)}, u32[]{:S(2)}) copy-start(f32[24,64]{1,0:T(8,128)S(1)} %broadcast_multiply_fusion.4) | copy-start | bytes 18436
  13.1 16.1 %copy-start.42 = (f32[24,64]{1,0:T(8,128)}, f32[24,64]{1,0:T(8,128)S(1)}, u32[]{:S(2)}) copy-start(f32[24,64]{1,0:T(8,128)S(1)} %add_rsqrt_fusion.1) | copy-start | bytes 18436
  13.2 16.0 %copy-start.36 = (f32[1,1024]{1,0:T(1,128)}, f32[1,1024]{1,0:T(1,128)S(1)}, u32[]{:S(2)}) copy-start(f32[1,1024]{1,0:T(1,128)S(1)} %get-tuple-element.74) | copy-start | bytes 12292
  13.2 564.2 %copy-start.34 = (f32[1,1024]{1,0:T(1,128)}, f32[1,1024]{1,0:T(1,128)S(1)}, u32[]{:S(2)}) copy-start(f32[1,1024]{1,0:T(1,128)S(1)} %get-tuple-element.72) | copy-start | bytes 12292
  13.8 15.4 %copy-start.45 = (f32[1,1024]{1,0:T(1,128)}, f32[1,1024]{1,0:T(1,128)S(1)}, u32[]{:S(2)}) copy-start(f32[1,1024]{1,0:T(1,128)S(1)} %get-tuple-element.77) | copy-start | bytes 12292
  33.0 20.2 %copy-start.13 = (bf16[24,64,128]{1,2,0:T(8,128)(2,1)}, bf16[24,64,128]{1,2,0:T(8,128)(2,1)S(1)}, u32[]{:S(2)}) copy-start(bf16[24,64,128]{1,2,0:T(8,128)(2,1)S(1)} %copy.81) | copy-start | bytes 1179652
  65.6 130.0 %copy-start.48 = (f32[1,1024]{1,0:T(1,128)S(1)}, f32[1,1024]{1,0:T(1,128)}, u32[]{:S(2)}) copy-start(f32[1,1024]{1,0:T(1,128)} %get-tuple-element.75) | copy-start | bytes 12292
  65.6 282.5 %all-reduce.5.cloned.1.call-start = ((), (), s32[]{:S(2)}) async-start(), calls=%async_computation.11 | async-start | bytes 6291456 | tf_op jit(solution)/shard_map/psum | solution.py:108
  201.3 14.9 %copy-start.12 = (bf16[24,64,1024]{2,1,0:T(8,128)(2,1)S(1)}, bf16[24,64,1024]{2,1,0:T(8,128)(2,1)}, u32[]{:S(2)}) copy-start(bf16[24,64,1024]{2,1,0:T(8,128)(2,1)} %param.23) | copy-start | bytes 9437188
  201.3 14.8 %copy-start.51 = (bf16[1024,1024]{1,0:T(8,128)(2,1)S(1)}, bf16[1024,1024]{1,0:T(8,128)(2,1)}, u32[]{:S(2)}) copy-start(bf16[1024,1024]{1,0:T(8,128)(2,1)} %param.20) | copy-start | bytes 6291460
  227.8 339.0 %all-gather.3.cloned.1.call-start = ((), (), s32[]{:S(2)}) async-start(), calls=%async_computation.20 | async-start | bytes 15728640 | tf_op jit(solution)/shard_map/all_gather | solution.py:13
  235.6 431.5 %reduce-scatter.15.cloned.1.call-start = ((), (), s32[]{:S(2)}) async-start(), calls=%async_computation.12 | async-start | bytes 3932160 | tf_op jit(solution)/shard_map/reduce_scatter | solution.py:178
  577.4 11.2 copy-start.20
  608.3 272.8 %reduce-scatter.17.cloned.1.call-start = ((), (), s32[]{:S(2)}) async-start(), calls=%async_computation.13 | async-start | bytes 15728640 | tf_op jit(solution)/shard_map/reduce_scatter | solution.py:175
  624.8 311.6 %reduce-scatter.29.cloned.1.call-start = ((), (), s32[]{:S(2)}) async-start(), calls=%async_computation.19 | async-start | bytes 4718592 | tf_op jit(solution)/shard_map/reduce_scatter | solution.py:163
  633.2 441.3 %reduce-scatter.31.cloned.1.call-start = ((), (), s32[]{:S(2)}) async-start(), calls=%async_computation.21 | async-start | bytes 540672
  653.0 14.1 copy-start.37
  887.2 18.7 %copy-start.28 = (f32[24,64]{1,0:T(8,128)}, f32[24,64]{1,0:T(8,128)S(1)}, u32[]{:S(2)}) copy-start(f32[24,64]{1,0:T(8,128)S(1)} %get-tuple-element.78) | copy-start | bytes 18436
  887.2 18.7 %copy-start.30 = (f32[24,64]{1,0:T(8,128)}, f32[24,64]{1,0:T(8,128)S(1)}, u32[]{:S(2)}) copy-start(f32[24,64]{1,0:T(8,128)S(1)} %get-tuple-element.79) | copy-start | bytes 18436
  894.2 314.8 %reduce-scatter.33.cloned.1.call-start = ((), (), s32[]{:S(2)}) async-start(), calls=%async_computation.22 | async-start | bytes 540672
  895.3 365.1 %reduce-scatter.27.cloned.1.call-start = ((), (), s32[]{:S(2)}) async-start(), calls=%async_computation.18 | async-start | bytes 4718592 | tf_op jit(solution)/shard_map/reduce_scatter | solution.py:162
  906.0 392.1 %reduce-scatter.25.cloned.1.call-start = ((), (), s32[]{:S(2)}) async-start(), calls=%async_computation.17 | async-start | bytes 589824 | tf_op jit(solution)/shard_map/reduce_scatter | solution.py:161
  921.8 414.1 %reduce-scatter.23.cloned.1.call-start = ((), (), s32[]{:S(2)}) async-start(), calls=%async_computation.16 | async-start | bytes 589824 | tf_op jit(solution)/shard_map/reduce_scatter | solution.py:160
  925.9 12.6 copy-start.9
  925.9 15.9 %copy-start.40 = (f32[24,64]{1,0:T(8,128)S(1)}, f32[24,64]{1,0:T(8,128)}, u32[]{:S(2)}) copy-start(f32[24,64]{1,0:T(8,128)} %get-tuple-element.45) | copy-start | bytes 18436
  925.9 15.9 %copy-start.29 = (f32[24,64]{1,0:T(8,128)S(1)}, f32[24,64]{1,0:T(8,128)}, u32[]{:S(2)}) copy-start(f32[24,64]{1,0:T(8,128)} %copy-done.28) | copy-start | bytes 18436
  925.9 15.9 %copy-start.31 = (f32[24,64]{1,0:T(8,128)S(1)}, f32[24,64]{1,0:T(8,128)}, u32[]{:S(2)}) copy-start(f32[24,64]{1,0:T(8,128)} %copy-done.30) | copy-start | bytes 18436
  927.2 446.3 %reduce-scatter.21.cloned.1.call-start = ((), (), s32[]{:S(2)}) async-start(), calls=%async_computation.15 | async-start | bytes 589824 | tf_op jit(solution)/shard_map/reduce_scatter | solution.py:159
  927.8 483.6 %reduce-scatter.19.cloned.1.call-start = ((), (), s32[]{:S(2)}) async-start(), calls=%async_computation.14 | async-start | bytes 589824 | tf_op jit(solution)/shard_map/reduce_scatter | solution.py:158
  941.8 469.5 %copy-start.1 = (bf16[1024,1024]{1,0:T(8,128)(2,1)S(1)}, bf16[1024,1024]{1,0:T(8,128)(2,1)}, u32[]{:S(2)}) copy-start(bf16[1024,1024]{1,0:T(8,128)(2,1)} %param.19) | copy-start | bytes 6291460
  (37 other events, 225.2 us)
Sparse Core Ops, SparseCore 0:
  65.7 123.7 all-reduce.2
  228.0 120.0 all-reduce.4
  349.6 217.1 all-gather.2
  608.4 58.5 reduce-scatter.14
  669.3 211.7 reduce-scatter.16
  884.3 52.0 reduce-scatter.28
  938.7 135.8 reduce-scatter.30
  1076.8 132.0 reduce-scatter.32
  1212.9 47.4 reduce-scatter.26
  1263.9 34.0 reduce-scatter.24
  1301.7 34.1 reduce-scatter.22
  1339.4 34.1 reduce-scatter.20
  1377.2 34.1 reduce-scatter.18
